TPU v7x, 512 devices: a whole 4x4x16 slice. The times are simulated.
512 devices in a mesh: dp: 8 (over y, core), expert: 64 (over x, z).
Axes of the slice: x: 4, y: 4, z: 16, core: 2. Of those that a mesh axis runs over, the one named last changes fastest.
Arguments:
- layer_in: bfloat16 [2048, 4096], P('expert', 'dp'), may hold values from -6 to 6
- grad_out: bfloat16 [2048, 4096], P('expert', 'dp'), may hold values from -6 to 6
- gate_prob: float32 [2048, 8], P('expert'), may hold values from 0.05 to 0.6
- expert_ids: int32 [2048, 8], P('expert'), may hold values from 0 to 31, as said below
- replica_index: int32 [2048, 8], P('expert'), may hold values from 0 to 3, as said below
- slot_expert: int32 [64], replicated, may hold values from 0 to 31, as said below
- w_gate: bfloat16 [64, 4096, 1024], P('expert', None, 'dp')
- w_up: bfloat16 [64, 4096, 1024], P('expert', None, 'dp')
- w_down: bfloat16 [64, 1024, 4096], P('expert', 'dp')
Outputs:
- grad_in: bfloat16 [2048, 4096], P('expert', 'dp')
- grad_w_down: bfloat16 [64, 1024, 4096], P('expert', 'dp')
Inputs may be any that keep to these rules, and one draw needn't show every extreme that they name: `slot_expert`: every expert owns one run of consecutive slots, counted cyclically (slot 63 is followed by slot 0), of 1 to 4 slots; the runs cover all 64 slots. `expert_ids`: the 8 experts of one token are different. `replica_index`: each entry is below the number of slots of the expert of the same choice. Of the 32 tokens of one index of expert, at most 8 choices go to any one slot, and in every draw some slot receives exactly 8 from the tokens of every index of expert.
All inputs are finite; a program needn't handle non-finite values.
Results may differ from a plain program's by a relative error of at most 0.014.
Values may be sent and summed in bfloat16 or wider, within the bound.
No kernel may reach another device: no remote copies, remote signals or barrier semaphores. Data moves between devices by JAX's collectives and lax.ppermute only.
A program may use at most 64 MiB of HBM per device.

v0:
```python
import jax
import jax.numpy as jnp
from jax import lax
from jax.sharding import PartitionSpec as P

TOP = 8


def passed_along(value, axis, steps):
    count = lax.axis_size(axis)
    pairs = [(source, (source + steps) % count) for source in range(count)]
    return lax.ppermute(value, axis, pairs)


def body(
    layer_in, grad_out, gate_prob, expert_ids, replica_index, slot_expert, w_gate, w_up, w_down
):
    slots = lax.axis_size("expert")
    maxrep = min(4, slots // 8)
    tok_count = layer_in.shape[0]
    capacity = tok_count // maxrep
    recv_rows = slots * capacity
    expert_count = (8 - maxrep) * slots // 8
    slot_index = jnp.arange(slots, dtype=jnp.int32)
    expert_index = jnp.arange(expert_count, dtype=jnp.int32)
    is_start = slot_expert != jnp.roll(slot_expert, 1)
    first_slot = jnp.sum(
        jnp.where(
            (slot_expert[None, :] == expert_index[:, None]) & is_start[None, :],
            slot_index[None, :],
            0,
        ),
        axis=1,
    )
    expert_flat = expert_ids.reshape(-1)
    route_slot = jnp.sum(
        jnp.where(expert_flat[:, None] == expert_index[None, :], first_slot[None, :], 0), axis=1
    )
    route_slot = (route_slot + replica_index.reshape(-1)) % slots
    onehot = (route_slot[:, None] == slot_index[None, :]).astype(jnp.int32)
    rank_in_slot = jnp.sum((jnp.cumsum(onehot, axis=0) - onehot) * onehot, axis=1)
    position = route_slot * capacity + rank_in_slot
    prob_flat = gate_prob.reshape(-1)

    def pack(values):
        buffer = jnp.zeros((recv_rows, values.shape[1]), values.dtype).at[position].set(values)
        return buffer.reshape(slots, capacity, values.shape[1])

    repeated = jnp.repeat(grad_out, TOP, axis=0).astype(jnp.float32)
    inputs, scaled = (
        lax.all_gather(
            lax.all_to_all(
                pack(jnp.repeat(layer_in, TOP, axis=0)),
                "expert",
                split_axis=0,
                concat_axis=0,
                tiled=True,
            ),
            "dp",
            axis=2,
            tiled=True,
        ),
        lax.all_gather(
            lax.all_to_all(
                pack((prob_flat[:, None] * repeated).astype(jnp.bfloat16)),
                "expert",
                split_axis=0,
                concat_axis=0,
                tiled=True,
            ),
            "dp",
            axis=2,
            tiled=True,
        ),
    )
    inputs = inputs.reshape(recv_rows, -1)
    scaled = scaled.reshape(recv_rows, -1)
    width = inputs.shape[1]
    gate_matrix = w_gate[0]
    up_matrix = w_up[0]
    down_matrix = w_down[0]
    gate_pre = jnp.dot(inputs, gate_matrix, preferred_element_type=jnp.float32)
    up_pre = jnp.dot(inputs, up_matrix, preferred_element_type=jnp.float32)
    hidden = (jax.nn.silu(gate_pre) * up_pre).astype(jnp.bfloat16)
    contract_last = (((1,), (1,)), ((), ()))
    hidden_grad = lax.dot_general(
        scaled, down_matrix, contract_last, preferred_element_type=jnp.float32
    )
    sigma = jax.nn.sigmoid(gate_pre)
    gate_grad = (hidden_grad * up_pre * sigma * (1.0 + gate_pre * (1.0 - sigma))).astype(
        jnp.bfloat16
    )
    up_grad = (hidden_grad * gate_pre * sigma).astype(jnp.bfloat16)
    partial_value = lax.dot_general(
        gate_grad, gate_matrix, contract_last, preferred_element_type=jnp.float32
    )
    partial_value = partial_value + lax.dot_general(
        up_grad, up_matrix, contract_last, preferred_element_type=jnp.float32
    )
    partial_value = partial_value.reshape(slots, capacity, width)
    summed = lax.psum_scatter(
        partial_value.astype(jnp.bfloat16), "dp", scatter_dimension=2, tiled=True
    ).astype(jnp.float32)
    returned = lax.all_to_all(
        summed.astype(jnp.bfloat16), "expert", split_axis=0, concat_axis=0, tiled=True
    ).astype(summed.dtype)
    flat_back = returned.reshape(recv_rows, -1)
    grad_in = jnp.sum(flat_back[position].reshape(tok_count, TOP, -1), axis=1).astype(jnp.bfloat16)
    slot_partial = lax.dot_general(
        hidden, scaled, (((0,), (0,)), ((), ())), preferred_element_type=jnp.float32
    ).astype(jnp.bfloat16)
    own_index = lax.axis_index("expert")
    expert_here = jnp.sum(jnp.where(slot_index == own_index, slot_expert, 0))

    def same_at(offset):
        neighbour = (own_index - offset) % slots
        match = jnp.any((slot_index == neighbour) & (slot_expert == expert_here))
        return match.astype(jnp.float32)

    total = slot_partial.astype(jnp.float32)
    for distance in range(1, maxrep):
        from_left = passed_along(slot_partial, "expert", distance)
        from_right = passed_along(slot_partial, "expert", -distance)
        total = (
            total
            + same_at(distance) * from_left.astype(jnp.float32)
            + same_at(-distance) * from_right.astype(jnp.float32)
        )
    grad_w_down = total.astype(jnp.bfloat16)[None]
    return (grad_in, grad_w_down)


def solution(mesh):
    placed = (
        P("expert", "dp"),
        P("expert", "dp"),
        P("expert", None),
        P("expert", None),
        P("expert", None),
        P(),
        P("expert", None, "dp"),
        P("expert", None, "dp"),
        P("expert", "dp", None),
    )
    return jax.shard_map(
        body,
        mesh=mesh,
        in_specs=placed,
        out_specs=(P("expert", "dp"), P("expert", "dp", None)),
        check_vma=False,
    )
```

profile of v0, /device:TPU:32, one launch (start us, length us, event | category | flops | bytes accessed | tf_op | source)
XLA Modules:
  0.0 336.8 jit_solution(1470478465016000383)
XLA Ops:
  7.2 0.0 copy-start
  7.2 0.0 copy-start.4
  7.2 0.0 copy-start.5
  7.2 0.0 all-gather.5.cloned.1.call-start
  7.2 0.8 copy.18
  8.1 0.1 reshape.135
  8.2 0.1 reshape.134
  8.3 0.1 reshape.133
  8.4 1.2 slice.14
  9.6 1.3 fusion.38
  10.9 2.1 broadcast_compare_fusion
  13.0 0.8 select_reduce_fusion.1
  13.8 0.8 copy.17
  14.5 0.1 eq.116
  14.6 0.1 select_reduce_fusion
  14.7 0.6 reduce-window.6
  15.4 0.2 slice_reduce_fusion
  15.6 0.1 fusion.30
  15.7 1.9 scatter_custom_fusion.1
  17.6 49.0 %all_to_all.15 = bf16[64,8,512]{2,1,0:T(8,128)(2,1)} all-to-all(bf16[64,8,512]{2,1,0:T(8,128)(2,1)S(1)} %bitcast.69), channel_id=1, replica_groups=mesh['dp'=8,'expert'=64] {'expert'}, dimensions={0} | all-to-all | bytes 1048576 | tf_op jit(solution)/shard_map/all_to_all | solution.py:52
  66.6 0.0 all-gather.5.cloned.1.call-update
  66.7 0.0 all-gather.3.cloned.1.call-start
  66.7 0.0 copy-done.4
  66.7 0.0 copy-done.5
  66.7 0.1 copy.22
  66.8 0.1 mul.90
  66.9 1.7 scatter_custom_fusion
  68.7 38.0 %all_to_all.16 = bf16[64,8,512]{2,1,0:T(8,128)(2,1)} all-to-all(bf16[64,8,512]{2,1,0:T(8,128)(2,1)S(1)} %bitcast.70), channel_id=1, replica_groups=mesh['dp'=8,'expert'=64] {'expert'}, dimensions={0} | all-to-all | bytes 1048576 | tf_op jit(solution)/shard_map/all_to_all | solution.py:64
  106.7 0.0 all-gather.3.cloned.1.call-update
  106.7 0.0 copy-start.2
  106.7 0.0 reduce-scatter.2.cloned.1.call-start
  106.7 0.0 all-gather.5.cloned.1.call-done
  106.8 0.0 copy-done
  106.8 0.0 copy-start.1
  106.8 3.6 %fusion.1 = f32[512,128]{1,0:T(8,128)S(1)} fusion(bf16[64,8,4096]{2,1,0:T(8,128)(2,1)} %all-gather.5.cloned.1.call-done, bf16[1,4096,128]{2,1,0:T(8,128)(2,1)S(1)} %copy-done), kind=kOutput, calls=%fused_computation.6 | convolution fusion | flops 536870912 | bytes 5505024 | tf_op jit(solution)/shard_map/dot_general | solution.py:82
  110.4 0.1 copy-done.1
  110.5 1.3 fusion.3
  111.7 30.4 %all-gather.3.cloned.1.call-done = bf16[64,8,4096]{2,1,0:T(8,128)(2,1)} async-done(((bf16[64,8,512]{2,1,0:T(8,128)(2,1)}), bf16[64,8,4096]{2,1,0:T(8,128)(2,1)}) %all-gather.3.cloned.1.call-update) | async-done | bytes 4194320 | tf_op jit(solution)/shard_map/all_gather | solution.py:63
  142.2 3.7 %fusion.6 = f32[512,128]{1,0:T(8,128)S(1)} fusion(bf16[64,8,4096]{2,1,0:T(8,128)(2,1)} %all-gather.3.cloned.1.call-done, bf16[1,128,4096]{2,1,0:T(8,128)(2,1)} %param.17), kind=kOutput, calls=%fused_computation.11 | convolution fusion | flops 536870912 | bytes 5505024 | tf_op jit(solution)/shard_map/dot_general | solution.py:86
  145.9 1.3 fusion.8
  147.2 3.2 fusion
  150.4 0.0 reduce-scatter.2.cloned.1.call-update
  150.4 3.0 convolution_convert_fusion
  153.4 3.6 %collective-permute-start = (bf16[128,4096]{1,0:T(8,128)(2,1)S(1)}, bf16[128,4096]{1,0:T(8,128)(2,1)S(1)}, u32[]{:S(2)}, u32[]{:S(2)}) collective-permute-start(bf16[128,4096]{1,0:T(8,128)(2,1)S(1)} %convolution_convert_fusion), channel_id=1, source_target_pairs={{0,1},{1,2},{2,3},{3,4},{4,5},{5,6},{6,7},{7,8},{8,9},{9,10},{10,1... | collective-permute-start | bytes 3145736 | tf_op jit(solution)/shard_map/ppermute | solution.py:12
  157.1 2.4 collective-permute-start.1
  159.4 5.2 %collective-permute-start.2 = (bf16[128,4096]{1,0:T(8,128)(2,1)S(1)}, bf16[128,4096]{1,0:T(8,128)(2,1)}, u32[]{:S(2)}, u32[]{:S(2)}) collective-permute-start(bf16[128,4096]{1,0:T(8,128)(2,1)S(1)} %convolution_convert_fusion), channel_id=1, source_target_pairs={{0,2},{1,3},{2,4},{3,5},{4,6},{5,7},{6,8},{7,9},{8,10},{9,11},{10,... | collective-permute-start | bytes 3145736 | tf_op jit(solution)/shard_map/ppermute | solution.py:12
  164.6 4.9 %collective-permute-start.3 = (bf16[128,4096]{1,0:T(8,128)(2,1)S(1)}, bf16[128,4096]{1,0:T(8,128)(2,1)}, u32[]{:S(2)}, u32[]{:S(2)}) collective-permute-start(bf16[128,4096]{1,0:T(8,128)(2,1)S(1)} %convolution_convert_fusion), channel_id=1, source_target_pairs={{0,62},{1,63},{2,0},{3,1},{4,2},{5,3},{6,4},{7,5},{8,6},{9,7},{10,... | collective-permute-start | bytes 3145736 | tf_op jit(solution)/shard_map/ppermute | solution.py:12
  169.5 5.8 %collective-permute-start.4 = (bf16[128,4096]{1,0:T(8,128)(2,1)S(1)}, bf16[128,4096]{1,0:T(8,128)(2,1)}, u32[]{:S(2)}, u32[]{:S(2)}) collective-permute-start(bf16[128,4096]{1,0:T(8,128)(2,1)S(1)} %convolution_convert_fusion), channel_id=1, source_target_pairs={{0,3},{1,4},{2,5},{3,6},{4,7},{5,8},{6,9},{7,10},{8,11},{9,12},{10... | collective-permute-start | bytes 3145736 | tf_op jit(solution)/shard_map/ppermute | solution.py:12
  175.3 7.0 %collective-permute-done = bf16[128,4096]{1,0:T(8,128)(2,1)S(1)} collective-permute-done((bf16[128,4096]{1,0:T(8,128)(2,1)S(1)}, bf16[128,4096]{1,0:T(8,128)(2,1)S(1)}, u32[]{:S(2)}, u32[]{:S(2)}) %collective-permute-start) | collective-permute-done | bytes 1048608 | tf_op jit(solution)/shard_map/ppermute | solution.py:12
  182.3 1.0 copy-done.3
  183.3 8.3 %collective-permute-start.5 = (bf16[128,4096]{1,0:T(8,128)(2,1)S(1)}, bf16[128,4096]{1,0:T(8,128)(2,1)}, u32[]{:S(2)}, u32[]{:S(2)}) collective-permute-start(bf16[128,4096]{1,0:T(8,128)(2,1)S(1)} %convolution_convert_fusion), channel_id=1, source_target_pairs={{0,61},{1,62},{2,63},{3,0},{4,1},{5,2},{6,3},{7,4},{8,5},{9,6},{10... | collective-permute-start | bytes 3145736 | tf_op jit(solution)/shard_map/ppermute | solution.py:12
  191.6 4.8 %reduce-scatter.2.cloned.1.call-done = bf16[64,8,512]{2,1,0:T(8,128)(2,1)} async-done(((bf16[64,8,4096]{2,1,0:T(8,128)(2,1)}), bf16[64,8,512]{2,1,0:T(8,128)(2,1)}) %reduce-scatter.2.cloned.1.call-update) | async-done | bytes 524304 | tf_op jit(solution)/shard_map/reduce_scatter | solution.py:101
  196.4 16.3 %all-to-all-start.2 = ((bf16[64,8,512]{2,1,0:T(8,128)(2,1)}), bf16[64,8,512]{2,1,0:T(8,128)(2,1)S(1)}, u32[]{:S(2)}, u32[]{:S(2)}) async-start(bf16[64,8,512]{2,1,0:T(8,128)(2,1)} %reduce-scatter.2.cloned.1.call-done), calls=%async_computation.3 | async-start | bytes 1048576 | tf_op jit(solution)/shard_map/all_to_all | solution.py:104
  212.8 0.8 and_reduce_fusion.5
  217.3 0.0 collective-permute-done.1
  217.4 13.9 %collective-permute-done.2 = bf16[128,4096]{1,0:T(8,128)(2,1)} collective-permute-done((bf16[128,4096]{1,0:T(8,128)(2,1)S(1)}, bf16[128,4096]{1,0:T(8,128)(2,1)}, u32[]{:S(2)}, u32[]{:S(2)}) %collective-permute-start.2) | collective-permute-done | bytes 1048608 | tf_op jit(solution)/shard_map/ppermute | solution.py:12
  231.3 0.0 collective-permute-done.3
  231.3 68.1 %collective-permute-done.4 = bf16[128,4096]{1,0:T(8,128)(2,1)} collective-permute-done((bf16[128,4096]{1,0:T(8,128)(2,1)S(1)}, bf16[128,4096]{1,0:T(8,128)(2,1)}, u32[]{:S(2)}, u32[]{:S(2)}) %collective-permute-start.4) | collective-permute-done | bytes 1048608 | tf_op jit(solution)/shard_map/ppermute | solution.py:12
  299.4 8.3 %collective-permute-done.5 = bf16[128,4096]{1,0:T(8,128)(2,1)} collective-permute-done((bf16[128,4096]{1,0:T(8,128)(2,1)S(1)}, bf16[128,4096]{1,0:T(8,128)(2,1)}, u32[]{:S(2)}, u32[]{:S(2)}) %collective-permute-start.5) | collective-permute-done | bytes 1048608 | tf_op jit(solution)/shard_map/ppermute | solution.py:12
  307.7 5.1 %fusion.14 = bf16[1,128,4096]{2,1,0:T(8,128)(2,1)} fusion(bf16[128,4096]{1,0:T(8,128)(2,1)} %collective-permute-done.5, f32[]{:T(128)S(6)} %convert_element_type.106, bf16[128,4096]{1,0:T(8,128)(2,1)} %collective-permute-done.4, f32[]{:T(128)S(6)} %convert_element_type.104, bf16[128,4096]{1,0:T(8,128)(2,1)} %collective-permute-done.3, ...), kind=kLoop, calls=%fused_computation.20 | loop fusion | flops 10485760 | bytes 8388632 | tf_op jit(solution)/shard_map/broadcast_in_dim | solution.py:129
  312.9 15.5 %all-to-all-done.2 = bf16[64,8,512]{2,1,0:T(8,128)(2,1)S(1)} async-done(((bf16[64,8,512]{2,1,0:T(8,128)(2,1)}), bf16[64,8,512]{2,1,0:T(8,128)(2,1)S(1)}, u32[]{:S(2)}, u32[]{:S(2)}) %all-to-all-start.2) | async-done | bytes 524320 | tf_op jit(solution)/shard_map/all_to_all | solution.py:104
  328.4 0.1 bitcast_convert_fusion
  328.5 1.0 gather_fusion
  329.5 0.7 bitcast_reduce_fusion
  (10 shorter events, 0.1 us)
Async XLA Ops:
  7.2 99.6 %copy-start = (bf16[1,4096,128]{2,1,0:T(8,128)(2,1)S(1)}, bf16[1,4096,128]{2,1,0:T(8,128)(2,1)}, u32[]{:S(2)}) copy-start(bf16[1,4096,128]{2,1,0:T(8,128)(2,1)} %param.15) | copy-start | bytes 3145732
  7.2 59.5 %copy-start.4 = (bf16[32,512]{1,0:T(8,128)(2,1)S(1)}, bf16[32,512]{1,0:T(8,128)(2,1)}, u32[]{:S(2)}) copy-start(bf16[32,512]{1,0:T(8,128)(2,1)} %param.10) | copy-start | bytes 98308
  7.2 59.6 %copy-start.5 = (f32[32,8]{0,1:T(8,128)S(1)}, f32[32,8]{0,1:T(8,128)}, u32[]{:S(2)}) copy-start(f32[32,8]{0,1:T(8,128)} %param.11) | copy-start | bytes 3076
  7.2 99.6 %all-gather.5.cloned.1.call-start = ((), (), s32[]{:S(2)}) async-start(), calls=%async_computation.5 | async-start | bytes 4718592 | tf_op jit(solution)/shard_map/all_gather | solution.py:51
  66.7 75.5 %all-gather.3.cloned.1.call-start = ((), (), s32[]{:S(2)}) async-start(), calls=%async_computation.4 | async-start | bytes 4718592 | tf_op jit(solution)/shard_map/all_gather | solution.py:63
  106.7 3.7 %copy-start.2 = (bf16[1,4096,128]{2,1,0:T(8,128)(2,1)S(1)}, bf16[1,4096,128]{2,1,0:T(8,128)(2,1)}, u32[]{:S(2)}) copy-start(bf16[1,4096,128]{2,1,0:T(8,128)(2,1)} %param.16) | copy-start | bytes 3145732
  106.7 89.7 %reduce-scatter.2.cloned.1.call-start = ((), (), s32[]{:S(2)}) async-start(), calls=%async_computation.6 | async-start | bytes 4718592 | tf_op jit(solution)/shard_map/reduce_scatter | solution.py:101
  106.8 3.7 %copy-start.1 = (bf16[64,8,4096]{2,1,0:T(8,128)(2,1)S(1)}, bf16[64,8,4096]{2,1,0:T(8,128)(2,1)}, u32[]{:S(2)}) copy-start(bf16[64,8,4096]{2,1,0:T(8,128)(2,1)} %all-gather.5.cloned.1.call-done) | copy-start | bytes 12582916
  153.4 28.9 %collective-permute-start = (bf16[128,4096]{1,0:T(8,128)(2,1)S(1)}, bf16[128,4096]{1,0:T(8,128)(2,1)S(1)}, u32[]{:S(2)}, u32[]{:S(2)}) collective-permute-start(bf16[128,4096]{1,0:T(8,128)(2,1)S(1)} %convolution_convert_fusion), channel_id=1, source_target_pairs={{0,1},{1,2},{2,3},{3,4},{4,5},{5,6},{6,7},{7,8},{8,9},{9,10},{10,1... | collective-permute-start | bytes 3145736 | tf_op jit(solution)/shard_map/ppermute | solution.py:12
  157.1 60.3 %collective-permute-start.1 = (bf16[128,4096]{1,0:T(8,128)(2,1)S(1)}, bf16[128,4096]{1,0:T(8,128)(2,1)}, u32[]{:S(2)}, u32[]{:S(2)}) collective-permute-start(bf16[128,4096]{1,0:T(8,128)(2,1)S(1)} %convolution_convert_fusion), channel_id=1, source_target_pairs={{0,63},{1,0},{2,1},{3,2},{4,3},{5,4},{6,5},{7,6},{8,7},{9,8},{10,9... | collective-permute-start | bytes 3145736 | tf_op jit(solution)/shard_map/ppermute | solution.py:12
  159.4 71.9 %collective-permute-start.2 = (bf16[128,4096]{1,0:T(8,128)(2,1)S(1)}, bf16[128,4096]{1,0:T(8,128)(2,1)}, u32[]{:S(2)}, u32[]{:S(2)}) collective-permute-start(bf16[128,4096]{1,0:T(8,128)(2,1)S(1)} %convolution_convert_fusion), channel_id=1, source_target_pairs={{0,2},{1,3},{2,4},{3,5},{4,6},{5,7},{6,8},{7,9},{8,10},{9,11},{10,... | collective-permute-start | bytes 3145736 | tf_op jit(solution)/shard_map/ppermute | solution.py:12
  164.6 66.7 %collective-permute-start.3 = (bf16[128,4096]{1,0:T(8,128)(2,1)S(1)}, bf16[128,4096]{1,0:T(8,128)(2,1)}, u32[]{:S(2)}, u32[]{:S(2)}) collective-permute-start(bf16[128,4096]{1,0:T(8,128)(2,1)S(1)} %convolution_convert_fusion), channel_id=1, source_target_pairs={{0,62},{1,63},{2,0},{3,1},{4,2},{5,3},{6,4},{7,5},{8,6},{9,7},{10,... | collective-permute-start | bytes 3145736 | tf_op jit(solution)/shard_map/ppermute | solution.py:12
  169.5 129.9 %collective-permute-start.4 = (bf16[128,4096]{1,0:T(8,128)(2,1)S(1)}, bf16[128,4096]{1,0:T(8,128)(2,1)}, u32[]{:S(2)}, u32[]{:S(2)}) collective-permute-start(bf16[128,4096]{1,0:T(8,128)(2,1)S(1)} %convolution_convert_fusion), channel_id=1, source_target_pairs={{0,3},{1,4},{2,5},{3,6},{4,7},{5,8},{6,9},{7,10},{8,11},{9,12},{10... | collective-permute-start | bytes 3145736 | tf_op jit(solution)/shard_map/ppermute | solution.py:12
  182.3 1.0 copy-start.3
  183.3 124.4 %collective-permute-start.5 = (bf16[128,4096]{1,0:T(8,128)(2,1)S(1)}, bf16[128,4096]{1,0:T(8,128)(2,1)}, u32[]{:S(2)}, u32[]{:S(2)}) collective-permute-start(bf16[128,4096]{1,0:T(8,128)(2,1)S(1)} %convolution_convert_fusion), channel_id=1, source_target_pairs={{0,61},{1,62},{2,63},{3,0},{4,1},{5,2},{6,3},{7,4},{8,5},{9,6},{10... | collective-permute-start | bytes 3145736 | tf_op jit(solution)/shard_map/ppermute | solution.py:12
  196.4 132.0 %all-to-all-start.2 = ((bf16[64,8,512]{2,1,0:T(8,128)(2,1)}), bf16[64,8,512]{2,1,0:T(8,128)(2,1)S(1)}, u32[]{:S(2)}, u32[]{:S(2)}) async-start(bf16[64,8,512]{2,1,0:T(8,128)(2,1)} %reduce-scatter.2.cloned.1.call-done), calls=%async_computation.3 | async-start | bytes 1048576 | tf_op jit(solution)/shard_map/all_to_all | solution.py:104
Sparse Core Ops, SparseCore 0:
  66.8 33.3 all-gather.4
  106.8 35.3 all-gather.2
  150.5 45.7 reduce-scatter.1
where the time goes:
time: 337 us
  waiting for transfers between devices  148 us (44%)
  blocking collectives  87 us (26%)
  starting transfers between devices  46.6 us (14%)
  between operations  17.9 us (5%)
  matrix products  16 us (5%)
  other arithmetic  13.6 us (4%)
  local copies, waits for them, and re-layouts  7.5 us (2%)
    ppermute x6, waiting for transfers between devices, passed_along(): return lax.ppermute(value, axis, pairs)  97.4 us
    all_to_all x1, blocking collectives, body(): lax.all_to_all(pack(jnp.repeat(layer_in, TOP, axis=0)), 'expert', split_a...  49 us
    all_to_all x1, blocking collectives, body(): lax.all_to_all(pack((prob_flat[:, None] * repeated).astype(jnp.bfloat16))...  38 us
    all_gather x1, waiting for transfers between devices, body(): lax.all_gather(lax.all_to_all(pack((prob_flat[:, None] * repeated).astype...  30.4 us
    ppermute x6, starting transfers between devices, passed_along(): return lax.ppermute(value, axis, pairs)  30.1 us
    all_to_all x1, starting transfers between devices, body(): lax.all_to_all(summed.astype(jnp.bfloat16), 'expert', split_axis=0, conca...  16.3 us
    all_to_all x1, waiting for transfers between devices, body(): lax.all_to_all(summed.astype(jnp.bfloat16), 'expert', split_axis=0, conca...  15.5 us
  transfers between devices with their start and end apart: 10, of which 7 were waited for; matrix products, arithmetic and copies ran while one was open for 5% of the time, Pallas kernels for 0%

commit v1 on v0

--- a/solution.py
+++ b/solution.py
@@ -1,9 +1,33 @@
+import functools
 import jax
 import jax.numpy as jnp
 from jax import lax
 from jax.sharding import PartitionSpec as P
 
 TOP = 8
+
+
+def advance_series_all_now(point, mesh_dim, axis_k):
+    n_parts = lax.axis_size(mesh_dim)
+    panels = []
+    for q in range(n_parts):
+        panels.append((q, (q + 1) % n_parts))
+    chunks = []
+    for q in range(n_parts):
+        chunks.append((q, (q - 1) % n_parts))
+    field_out, val2 = ([point], [point])
+    for _ in range(n_parts // 2):
+        top = lax.ppermute(field_out[-1], axis_name=mesh_dim, perm=panels)
+        field_out.append(top)
+    for _ in range((n_parts - 1) // 2):
+        u1 = lax.ppermute(val2[-1], mesh_dim, chunks)
+        val2.append(u1)
+    w_next = jnp.concatenate([*field_out[::-1], *val2[1:]], axis_k)
+    met_up = lax.axis_index(mesh_dim)
+    return jnp.roll(w_next, (met_up - n_parts // 2) * point.shape[axis_k], axis_k)
+
+
+point_the_ends = functools.partial(advance_series_all_now, mesh_dim="dp", axis_k=2)
 
 
 def passed_along(value, axis, steps):
@@ -60,17 +84,14 @@
             axis=2,
             tiled=True,
         ),
-        lax.all_gather(
+        point_the_ends(
             lax.all_to_all(
                 pack((prob_flat[:, None] * repeated).astype(jnp.bfloat16)),
                 "expert",
                 split_axis=0,
                 concat_axis=0,
                 tiled=True,
-            ),
-            "dp",
-            axis=2,
-            tiled=True,
+            )
         ),
     )
     inputs = inputs.reshape(recv_rows, -1)

time: 337 us -> 352 us (1.045)
  the two profiles are of different devices: /device:TPU:32 before, /device:TPU:25 now
where the time goes in v1:
time: 352 us; the launch traced here: 351 us
  waiting for transfers between devices  142 us (40%)
  blocking collectives  84.4 us (24%)
  starting transfers between devices  57.3 us (16%)
  local copies, waits for them, and re-layouts  18.8 us (5%)
  between operations  18.3 us (5%)
  matrix products  15.6 us (4%)
  other arithmetic  14.3 us (4%)
    ppermute x6, waiting for transfers between devices, passed_along(): return lax.ppermute(value, axis, pairs)  96.2 us
    all_to_all x1, blocking collectives, body(): lax.all_to_all(pack(jnp.repeat(layer_in, TOP, axis=0)), 'expert', split_a...  47.6 us
    all_to_all x1, blocking collectives, body(): lax.all_to_all(pack((prob_flat[:, None] * repeated).astype(jnp.bfloat16))...  36.9 us
    ppermute x6, starting transfers between devices, passed_along(): return lax.ppermute(value, axis, pairs)  26.7 us
    ppermute x4, waiting for transfers between devices, advance_series_all_now(): top = lax.ppermute(field_out[-1], axis_name=mesh_dim, perm=panels)  24.8 us
    all_to_all x1, waiting for transfers between devices, body(): lax.all_to_all(summed.astype(jnp.bfloat16), 'expert', split_axis=0, conca...  21.2 us
    all_to_all x1, starting transfers between devices, body(): lax.all_to_all(summed.astype(jnp.bfloat16), 'expert', split_axis=0, conca...  15.6 us
    ppermute x4, starting transfers between devices, advance_series_all_now(): top = lax.ppermute(field_out[-1], axis_name=mesh_dim, perm=panels)  15 us
  transfers between devices with their start and end apart: 16, of which 9 were waited for; matrix products, arithmetic and copies ran while one was open for 6% of the time, Pallas kernels for 0%

profile of v1, /device:TPU:25, one launch (start us, length us, event | category | flops | bytes accessed | tf_op | source)
XLA Modules:
  0.0 351.0 jit_solution(17770139020133627076)
XLA Ops:
  7.2 0.8 copy.18
  8.1 0.1 reshape.135
  8.2 0.1 reshape.134
  8.2 0.1 reshape.133
  8.3 1.2 slice.14
  9.6 1.3 fusion.40
  10.9 2.1 broadcast_compare_fusion
  13.0 0.8 select_reduce_fusion.1
  13.7 0.8 copy.17
  14.5 0.1 eq.119
  14.6 0.1 select_reduce_fusion
  14.7 0.6 reduce-window.6
  15.3 0.2 slice_reduce_fusion
  15.6 0.1 fusion.32
  15.7 1.9 scatter_custom_fusion.1
  17.6 47.6 %all_to_all.15 = bf16[64,8,512]{2,1,0:T(8,128)(2,1)} all-to-all(bf16[64,8,512]{2,1,0:T(8,128)(2,1)S(1)} %bitcast.69), channel_id=1, replica_groups=mesh['dp'=8,'expert'=64] {'expert'}, dimensions={0} | all-to-all | bytes 1048576 | tf_op jit(solution)/shard_map/all_to_all | solution.py:76
  65.2 0.8 convert_element_type.85
  66.0 0.8 copy.22
  66.8 0.1 mul.93
  66.9 1.7 scatter_custom_fusion
  68.6 36.9 %all_to_all.16 = bf16[64,8,512]{2,1,0:T(8,128)(2,1)S(1)} all-to-all(bf16[64,8,512]{2,1,0:T(8,128)(2,1)S(1)} %bitcast.70), channel_id=1, replica_groups=mesh['dp'=8,'expert'=64] {'expert'}, dimensions={0} | all-to-all | bytes 1048576 | tf_op jit(solution)/shard_map/all_to_all | solution.py:88
  105.5 3.8 %collective-permute-start = (bf16[64,8,512]{2,1,0:T(8,128)(2,1)S(1)}, bf16[64,8,512]{2,1,0:T(8,128)(2,1)S(1)}, u32[]{:S(2)}, u32[]{:S(2)}) collective-permute-start(bf16[64,8,512]{2,1,0:T(8,128)(2,1)S(1)} %all_to_all.16), channel_id=1, source_target_pairs={{0,64},{64,128},{128,192},{192,256},{256,320},{320,384},{384,448},... | collective-permute-start | bytes 1572872 | tf_op jit(solution)/shard_map/ppermute | solution.py:20
  109.3 6.1 %collective-permute-done = bf16[64,8,512]{2,1,0:T(8,128)(2,1)S(1)} collective-permute-done((bf16[64,8,512]{2,1,0:T(8,128)(2,1)S(1)}, bf16[64,8,512]{2,1,0:T(8,128)(2,1)S(1)}, u32[]{:S(2)}, u32[]{:S(2)}) %collective-permute-start) | collective-permute-done | bytes 524320 | tf_op jit(solution)/shard_map/ppermute | solution.py:20
  115.4 3.7 %collective-permute-start.1 = (bf16[64,8,512]{2,1,0:T(8,128)(2,1)S(1)}, bf16[64,8,512]{2,1,0:T(8,128)(2,1)S(1)}, u32[]{:S(2)}, u32[]{:S(2)}) collective-permute-start(bf16[64,8,512]{2,1,0:T(8,128)(2,1)S(1)} %collective-permute-done), channel_id=1, source_target_pairs={{0,64},{64,128},{128,192},{192,256},{256,320},{320,384},{384,448},... | collective-permute-start | bytes 1572872 | tf_op jit(solution)/shard_map/ppermute | solution.py:20
  119.1 6.1 %collective-permute-done.1 = bf16[64,8,512]{2,1,0:T(8,128)(2,1)S(1)} collective-permute-done((bf16[64,8,512]{2,1,0:T(8,128)(2,1)S(1)}, bf16[64,8,512]{2,1,0:T(8,128)(2,1)S(1)}, u32[]{:S(2)}, u32[]{:S(2)}) %collective-permute-start.1) | collective-permute-done | bytes 524320 | tf_op jit(solution)/shard_map/ppermute | solution.py:20
  125.2 3.7 %collective-permute-start.2 = (bf16[64,8,512]{2,1,0:T(8,128)(2,1)S(1)}, bf16[64,8,512]{2,1,0:T(8,128)(2,1)}, u32[]{:S(2)}, u32[]{:S(2)}) collective-permute-start(bf16[64,8,512]{2,1,0:T(8,128)(2,1)S(1)} %collective-permute-done.1), channel_id=1, source_target_pairs={{0,64},{64,128},{128,192},{192,256},{256,320},{320,384},{384,448},... | collective-permute-start | bytes 1572872 | tf_op jit(solution)/shard_map/ppermute | solution.py:20
  128.9 6.1 %collective-permute-done.2 = bf16[64,8,512]{2,1,0:T(8,128)(2,1)} collective-permute-done((bf16[64,8,512]{2,1,0:T(8,128)(2,1)S(1)}, bf16[64,8,512]{2,1,0:T(8,128)(2,1)}, u32[]{:S(2)}, u32[]{:S(2)}) %collective-permute-start.2) | collective-permute-done | bytes 524320 | tf_op jit(solution)/shard_map/ppermute | solution.py:20
  135.0 3.8 %collective-permute-start.3 = (bf16[64,8,512]{2,1,0:T(8,128)(2,1)}, bf16[64,8,512]{2,1,0:T(8,128)(2,1)}, u32[]{:S(2)}, u32[]{:S(2)}) collective-permute-start(bf16[64,8,512]{2,1,0:T(8,128)(2,1)} %collective-permute-done.2), channel_id=1, source_target_pairs={{0,64},{64,128},{128,192},{192,256},{256,320},{320,384},{384,448},... | collective-permute-start | bytes 1572872 | tf_op jit(solution)/shard_map/ppermute | solution.py:20
  138.8 6.4 %collective-permute-done.3 = bf16[64,8,512]{2,1,0:T(8,128)(2,1)} collective-permute-done((bf16[64,8,512]{2,1,0:T(8,128)(2,1)}, bf16[64,8,512]{2,1,0:T(8,128)(2,1)}, u32[]{:S(2)}, u32[]{:S(2)}) %collective-permute-start.3) | collective-permute-done | bytes 524320 | tf_op jit(solution)/shard_map/ppermute | solution.py:20
  145.3 1.1 constant_dynamic-update-slice_fusion.15
  146.4 1.1 constant_dynamic-update-slice_fusion.14
  147.5 0.1 constant_dynamic-update-slice_fusion.13
  147.7 0.1 constant_dynamic-update-slice_fusion.11
  147.7 0.1 constant_dynamic-update-slice_fusion.10
  147.8 1.1 constant_dynamic-update-slice_fusion.9
  149.0 1.1 constant_dynamic-update-slice_fusion.7
  150.1 1.1 constant_dynamic-update-slice_fusion.6
  151.4 0.1 constant_dynamic-update-slice_fusion.3
  151.5 1.2 constant_dynamic-update-slice_fusion.2
  152.7 1.1 constant_dynamic-update-slice_fusion.1
  153.9 3.2 copy-done.1
  157.1 1.3 fusion.6
  158.4 3.4 fusion.1
  161.9 3.4 fusion.3
  165.3 1.3 fusion.10
  166.6 3.3 fusion
  169.8 3.0 convolution_convert_fusion
  172.8 5.0 %collective-permute-start.10 = (bf16[128,4096]{1,0:T(8,128)(2,1)S(1)}, bf16[128,4096]{1,0:T(8,128)(2,1)}, u32[]{:S(2)}, u32[]{:S(2)}) collective-permute-start(bf16[128,4096]{1,0:T(8,128)(2,1)S(1)} %convolution_convert_fusion), channel_id=1, source_target_pairs={{0,62},{1,63},{2,0},{3,1},{4,2},{5,3},{6,4},{7,5},{8,6},{9,7},{10,... | collective-permute-start | bytes 3145736 | tf_op jit(solution)/shard_map/ppermute | solution.py:36
  177.9 1.9 collective-permute-start.11
  179.8 8.5 %collective-permute-start.12 = (bf16[128,4096]{1,0:T(8,128)(2,1)S(1)}, bf16[128,4096]{1,0:T(8,128)(2,1)}, u32[]{:S(2)}, u32[]{:S(2)}) collective-permute-start(bf16[128,4096]{1,0:T(8,128)(2,1)S(1)} %convolution_convert_fusion), channel_id=1, source_target_pairs={{0,61},{1,62},{2,63},{3,0},{4,1},{5,2},{6,3},{7,4},{8,5},{9,6},{10... | collective-permute-start | bytes 3145736 | tf_op jit(solution)/shard_map/ppermute | solution.py:36
  188.3 1.9 collective-permute-start.7
  190.2 6.7 %collective-permute-start.8 = (bf16[128,4096]{1,0:T(8,128)(2,1)S(1)}, bf16[128,4096]{1,0:T(8,128)(2,1)}, u32[]{:S(2)}, u32[]{:S(2)}) collective-permute-start(bf16[128,4096]{1,0:T(8,128)(2,1)S(1)} %convolution_convert_fusion), channel_id=1, source_target_pairs={{0,63},{1,0},{2,1},{3,2},{4,3},{5,4},{6,5},{7,6},{8,7},{9,8},{10,9... | collective-permute-start | bytes 3145736 | tf_op jit(solution)/shard_map/ppermute | solution.py:36
  196.9 27.5 %collective-permute-done.10 = bf16[128,4096]{1,0:T(8,128)(2,1)} collective-permute-done((bf16[128,4096]{1,0:T(8,128)(2,1)S(1)}, bf16[128,4096]{1,0:T(8,128)(2,1)}, u32[]{:S(2)}, u32[]{:S(2)}) %collective-permute-start.10) | collective-permute-done | bytes 1048608 | tf_op jit(solution)/shard_map/ppermute | solution.py:36
  224.4 2.6 collective-permute-start.9
  227.0 15.6 %all-to-all-start.2 = ((bf16[64,8,512]{2,1,0:T(8,128)(2,1)}), bf16[64,8,512]{2,1,0:T(8,128)(2,1)S(1)}, u32[]{:S(2)}, u32[]{:S(2)}) async-start(bf16[64,8,512]{2,1,0:T(8,128)(2,1)} %reduce-scatter.2.cloned.1.call-done), calls=%async_computation.3 | async-start | bytes 1048576 | tf_op jit(solution)/shard_map/all_to_all | solution.py:125
  242.7 0.8 and_reduce_fusion.5
  247.3 5.9 %collective-permute-done.11 = bf16[128,4096]{1,0:T(8,128)(2,1)} collective-permute-done((bf16[128,4096]{1,0:T(8,128)(2,1)S(1)}, bf16[128,4096]{1,0:T(8,128)(2,1)}, u32[]{:S(2)}, u32[]{:S(2)}) %collective-permute-start.11) | collective-permute-done | bytes 1048608 | tf_op jit(solution)/shard_map/ppermute | solution.py:36
  253.1 36.7 %collective-permute-done.12 = bf16[128,4096]{1,0:T(8,128)(2,1)} collective-permute-done((bf16[128,4096]{1,0:T(8,128)(2,1)S(1)}, bf16[128,4096]{1,0:T(8,128)(2,1)}, u32[]{:S(2)}, u32[]{:S(2)}) %collective-permute-start.12) | collective-permute-done | bytes 1048608 | tf_op jit(solution)/shard_map/ppermute | solution.py:36
  289.9 26.0 %collective-permute-done.8 = bf16[128,4096]{1,0:T(8,128)(2,1)} collective-permute-done((bf16[128,4096]{1,0:T(8,128)(2,1)S(1)}, bf16[128,4096]{1,0:T(8,128)(2,1)}, u32[]{:S(2)}, u32[]{:S(2)}) %collective-permute-start.8) | collective-permute-done | bytes 1048608 | tf_op jit(solution)/shard_map/ppermute | solution.py:36
  315.9 5.1 %fusion.16 = bf16[1,128,4096]{2,1,0:T(8,128)(2,1)} fusion(bf16[128,4096]{1,0:T(8,128)(2,1)} %collective-permute-done.12, f32[]{:T(128)S(6)} %convert_element_type.106, bf16[128,4096]{1,0:T(8,128)(2,1)} %collective-permute-done.11, f32[]{:T(128)S(6)} %convert_element_type.104, bf16[128,4096]{1,0:T(8,128)(2,1)} %collective-permute-done.10, ...), kind=kLoop, calls=%fused_computation.22 | loop fusion | flops 10485760 | bytes 8388632 | tf_op jit(solution)/shard_map/broadcast_in_dim | solution.py:150
  321.0 21.2 %all-to-all-done.2 = bf16[64,8,512]{2,1,0:T(8,128)(2,1)S(1)} async-done(((bf16[64,8,512]{2,1,0:T(8,128)(2,1)}), bf16[64,8,512]{2,1,0:T(8,128)(2,1)S(1)}, u32[]{:S(2)}, u32[]{:S(2)}) %all-to-all-start.2) | async-done | bytes 524320 | tf_op jit(solution)/shard_map/all_to_all | solution.py:125
  342.3 0.1 bitcast_convert_fusion
  342.4 1.0 gather_fusion
  343.4 0.7 bitcast_reduce_fusion
  (35 shorter events, 0.6 us)
Async XLA Ops:
  7.2 151.2 %copy-start = (bf16[1,4096,128]{2,1,0:T(8,128)(2,1)S(1)}, bf16[1,4096,128]{2,1,0:T(8,128)(2,1)}, u32[]{:S(2)}) copy-start(bf16[1,4096,128]{2,1,0:T(8,128)(2,1)} %param.15) | copy-start | bytes 3145732
  7.2 151.2 %all-gather.2.cloned.1.call-start = ((), (), s32[]{:S(2)}) async-start(), calls=%async_computation.4 | async-start | bytes 4718592 | tf_op jit(solution)/shard_map/all_gather | solution.py:75
  65.2 161.8 %reduce-scatter.2.cloned.1.call-start = ((), (), s32[]{:S(2)}) async-start(), calls=%async_computation.5 | async-start | bytes 4718592 | tf_op jit(solution)/shard_map/reduce_scatter | solution.py:122
  105.5 10.0 %collective-permute-start = (bf16[64,8,512]{2,1,0:T(8,128)(2,1)S(1)}, bf16[64,8,512]{2,1,0:T(8,128)(2,1)S(1)}, u32[]{:S(2)}, u32[]{:S(2)}) collective-permute-start(bf16[64,8,512]{2,1,0:T(8,128)(2,1)S(1)} %all_to_all.16), channel_id=1, source_target_pairs={{0,64},{64,128},{128,192},{192,256},{256,320},{320,384},{384,448},... | collective-permute-start | bytes 1572872 | tf_op jit(solution)/shard_map/ppermute | solution.py:20
  115.4 9.8 %collective-permute-start.1 = (bf16[64,8,512]{2,1,0:T(8,128)(2,1)S(1)}, bf16[64,8,512]{2,1,0:T(8,128)(2,1)S(1)}, u32[]{:S(2)}, u32[]{:S(2)}) collective-permute-start(bf16[64,8,512]{2,1,0:T(8,128)(2,1)S(1)} %collective-permute-done), channel_id=1, source_target_pairs={{0,64},{64,128},{128,192},{192,256},{256,320},{320,384},{384,448},... | collective-permute-start | bytes 1572872 | tf_op jit(solution)/shard_map/ppermute | solution.py:20
  119.1 9.8 %collective-permute-start.4 = (bf16[64,8,512]{2,1,0:T(8,128)(2,1)S(1)}, bf16[64,8,512]{2,1,0:T(8,128)(2,1)S(1)}, u32[]{:S(2)}, u32[]{:S(2)}) collective-permute-start(bf16[64,8,512]{2,1,0:T(8,128)(2,1)S(1)} %all_to_all.16), channel_id=1, source_target_pairs={{0,448},{64,0},{128,64},{192,128},{256,192},{320,256},{384,320},{4... | collective-permute-start | bytes 1572872 | tf_op jit(solution)/shard_map/ppermute | solution.py:23
  125.2 9.8 %collective-permute-start.2 = (bf16[64,8,512]{2,1,0:T(8,128)(2,1)S(1)}, bf16[64,8,512]{2,1,0:T(8,128)(2,1)}, u32[]{:S(2)}, u32[]{:S(2)}) collective-permute-start(bf16[64,8,512]{2,1,0:T(8,128)(2,1)S(1)} %collective-permute-done.1), channel_id=1, source_target_pairs={{0,64},{64,128},{128,192},{192,256},{256,320},{320,384},{384,448},... | collective-permute-start | bytes 1572872 | tf_op jit(solution)/shard_map/ppermute | solution.py:20
  128.9 22.3 %copy-start.3 = (bf16[64,8,512]{2,1,0:T(8,128)(2,1)}, bf16[64,8,512]{2,1,0:T(8,128)(2,1)S(1)}, u32[]{:S(2)}) copy-start(bf16[64,8,512]{2,1,0:T(8,128)(2,1)S(1)} %collective-permute-done.4) | copy-start | bytes 1572868
  128.9 9.9 %collective-permute-start.5 = (bf16[64,8,512]{2,1,0:T(8,128)(2,1)S(1)}, bf16[64,8,512]{2,1,0:T(8,128)(2,1)}, u32[]{:S(2)}, u32[]{:S(2)}) collective-permute-start(bf16[64,8,512]{2,1,0:T(8,128)(2,1)S(1)} %collective-permute-done.4), channel_id=1, source_target_pairs={{0,448},{64,0},{128,64},{192,128},{256,192},{320,256},{384,320},{4... | collective-permute-start | bytes 1572872 | tf_op jit(solution)/shard_map/ppermute | solution.py:23
  135.0 10.2 %collective-permute-start.3 = (bf16[64,8,512]{2,1,0:T(8,128)(2,1)}, bf16[64,8,512]{2,1,0:T(8,128)(2,1)}, u32[]{:S(2)}, u32[]{:S(2)}) collective-permute-start(bf16[64,8,512]{2,1,0:T(8,128)(2,1)} %collective-permute-done.2), channel_id=1, source_target_pairs={{0,64},{64,128},{128,192},{192,256},{256,320},{320,384},{384,448},... | collective-permute-start | bytes 1572872 | tf_op jit(solution)/shard_map/ppermute | solution.py:20
  138.8 18.3 %copy-start.4 = (bf16[1,128,4096]{2,1,0:T(8,128)(2,1)S(1)}, bf16[1,128,4096]{2,1,0:T(8,128)(2,1)}, u32[]{:S(2)}) copy-start(bf16[1,128,4096]{2,1,0:T(8,128)(2,1)} %param.17) | copy-start | bytes 3145732
  138.8 10.1 %collective-permute-start.6 = (bf16[64,8,512]{2,1,0:T(8,128)(2,1)}, bf16[64,8,512]{2,1,0:T(8,128)(2,1)S(1)}, u32[]{:S(2)}, u32[]{:S(2)}) collective-permute-start(bf16[64,8,512]{2,1,0:T(8,128)(2,1)} %collective-permute-done.5), channel_id=1, source_target_pairs={{0,448},{64,0},{128,64},{192,128},{256,192},{320,256},{384,320},{4... | collective-permute-start | bytes 1572872 | tf_op jit(solution)/shard_map/ppermute | solution.py:23
  151.3 10.5 %copy-start.2 = (bf16[1,4096,128]{2,1,0:T(8,128)(2,1)S(1)}, bf16[1,4096,128]{2,1,0:T(8,128)(2,1)}, u32[]{:S(2)}) copy-start(bf16[1,4096,128]{2,1,0:T(8,128)(2,1)} %param.16) | copy-start | bytes 3145732
  153.9 3.2 copy-start.1
  172.8 51.5 %collective-permute-start.10 = (bf16[128,4096]{1,0:T(8,128)(2,1)S(1)}, bf16[128,4096]{1,0:T(8,128)(2,1)}, u32[]{:S(2)}, u32[]{:S(2)}) collective-permute-start(bf16[128,4096]{1,0:T(8,128)(2,1)S(1)} %convolution_convert_fusion), channel_id=1, source_target_pairs={{0,62},{1,63},{2,0},{3,1},{4,2},{5,3},{6,4},{7,5},{8,6},{9,7},{10,... | collective-permute-start | bytes 3145736 | tf_op jit(solution)/shard_map/ppermute | solution.py:36
  177.9 75.3 %collective-permute-start.11 = (bf16[128,4096]{1,0:T(8,128)(2,1)S(1)}, bf16[128,4096]{1,0:T(8,128)(2,1)}, u32[]{:S(2)}, u32[]{:S(2)}) collective-permute-start(bf16[128,4096]{1,0:T(8,128)(2,1)S(1)} %convolution_convert_fusion), channel_id=1, source_target_pairs={{0,3},{1,4},{2,5},{3,6},{4,7},{5,8},{6,9},{7,10},{8,11},{9,12},{10... | collective-permute-start | bytes 3145736 | tf_op jit(solution)/shard_map/ppermute | solution.py:36
  179.8 110.1 %collective-permute-start.12 = (bf16[128,4096]{1,0:T(8,128)(2,1)S(1)}, bf16[128,4096]{1,0:T(8,128)(2,1)}, u32[]{:S(2)}, u32[]{:S(2)}) collective-permute-start(bf16[128,4096]{1,0:T(8,128)(2,1)S(1)} %convolution_convert_fusion), channel_id=1, source_target_pairs={{0,61},{1,62},{2,63},{3,0},{4,1},{5,2},{6,3},{7,4},{8,5},{9,6},{10... | collective-permute-start | bytes 3145736 | tf_op jit(solution)/shard_map/ppermute | solution.py:36
  188.3 101.6 %collective-permute-start.7 = (bf16[128,4096]{1,0:T(8,128)(2,1)S(1)}, bf16[128,4096]{1,0:T(8,128)(2,1)}, u32[]{:S(2)}, u32[]{:S(2)}) collective-permute-start(bf16[128,4096]{1,0:T(8,128)(2,1)S(1)} %convolution_convert_fusion), channel_id=1, source_target_pairs={{0,1},{1,2},{2,3},{3,4},{4,5},{5,6},{6,7},{7,8},{8,9},{9,10},{10,1... | collective-permute-start | bytes 3145736 | tf_op jit(solution)/shard_map/ppermute | solution.py:36
  190.2 125.7 %collective-permute-start.8 = (bf16[128,4096]{1,0:T(8,128)(2,1)S(1)}, bf16[128,4096]{1,0:T(8,128)(2,1)}, u32[]{:S(2)}, u32[]{:S(2)}) collective-permute-start(bf16[128,4096]{1,0:T(8,128)(2,1)S(1)} %convolution_convert_fusion), channel_id=1, source_target_pairs={{0,63},{1,0},{2,1},{3,2},{4,3},{5,4},{6,5},{7,6},{8,7},{9,8},{10,9... | collective-permute-start | bytes 3145736 | tf_op jit(solution)/shard_map/ppermute | solution.py:36
  224.4 91.6 %collective-permute-start.9 = (bf16[128,4096]{1,0:T(8,128)(2,1)S(1)}, bf16[128,4096]{1,0:T(8,128)(2,1)}, u32[]{:S(2)}, u32[]{:S(2)}) collective-permute-start(bf16[128,4096]{1,0:T(8,128)(2,1)S(1)} %convolution_convert_fusion), channel_id=1, source_target_pairs={{0,2},{1,3},{2,4},{3,5},{4,6},{5,7},{6,8},{7,9},{8,10},{9,11},{10,... | collective-permute-start | bytes 3145736 | tf_op jit(solution)/shard_map/ppermute | solution.py:36
  227.0 115.2 %all-to-all-start.2 = ((bf16[64,8,512]{2,1,0:T(8,128)(2,1)}), bf16[64,8,512]{2,1,0:T(8,128)(2,1)S(1)}, u32[]{:S(2)}, u32[]{:S(2)}) async-start(bf16[64,8,512]{2,1,0:T(8,128)(2,1)} %reduce-scatter.2.cloned.1.call-done), calls=%async_computation.3 | async-start | bytes 1048576 | tf_op jit(solution)/shard_map/all_to_all | solution.py:125
Sparse Core Ops, SparseCore 0:
  65.3 33.4 all-gather.1
  170.0 38.8 reduce-scatter.1
